TPU v7x, 512 devices: a whole 4x8x8 slice. The times are simulated.
512 devices in a mesh: enc: 32 (over y, x), section: 8 (over z_lo, core), llmdp: 2 (over z_hi).
Axes of the slice: x: 4, y: 8, z: 8 (z_hi: 2, z_lo: 4; z = z_hi * 4 + z_lo), core: 2. Of those that a mesh axis runs over, the one named last changes fastest.
Arguments:
- patches: bfloat16 [8192, 3200], P('enc', ('section', 'llmdp')), may hold values from -6 to 6
- gain: float32 [3200], replicated, may hold values from 0.25 to 1.75
- shift: float32 [3200], replicated, may hold values from -3 to 3
- proj_weight: bfloat16 [3200, 8192], P('enc', ('section', 'llmdp')), may hold values from -0.109375 to 0.109375
- llm_rank: int32 [8192, 1], P('enc'), may hold values from 0 to 31; in each aligned block of 256 rows (0 to 255, 256 to 511, ...) at most 24 rows name the same one
- embed_grad: bfloat16 [24576, 8192], P('enc', ('section', 'llmdp')), may hold values from -0.59765625 to 0.59765625
Outputs:
- embeds_recv: bfloat16 [24576, 8192], P('enc', ('section', 'llmdp'))
- hidden_state_gradient: bfloat16 [8192, 3200], P('enc', ('section', 'llmdp'))
- grad_weight: float32 [3200, 8192], P('enc', ('section', 'llmdp'))
- gain_gradient: float32 [3200], P(('section', 'llmdp'))
- grad_shift: float32 [3200], P(('section', 'llmdp'))
Inputs may be any that keep to these rules, and one draw needn't show every extreme that they name: `llm_rank`: among the 256 rows of one device, at most 24 name the same owner, a bound that some block reaches.
All inputs are finite; a program needn't handle non-finite values.
Results may differ from a plain program's by a relative error of at most 0.018.
Values may be sent and summed in bfloat16 or wider, within the bound.
No kernel may reach another device: no remote copies, remote signals or barrier semaphores. Data moves between devices by JAX's collectives and lax.ppermute only.
A program may use at most 64 MiB of HBM per device.

v0:
```python
import jax
import jax.numpy as jnp
from jax import lax
from jax.sharding import Mesh
from jax.sharding import PartitionSpec as P

ENC = ("enc_0", "enc_1")
EPSILON = 1e-05


def whole_of(x, axes, dim):
    for axis in reversed(axes):
        x = lax.all_gather(x, axis, axis=dim, tiled=True)
    return x


def summed_rows(terms, axes):
    running = terms.astype(jnp.bfloat16)
    for axis in axes:
        running = lax.psum_scatter(running, axis, scatter_dimension=0, tiled=True)
    return running.astype(jnp.float32)


def copy_for_each(x, axis):
    peers = lax.axis_size(axis)
    return lax.all_to_all(jnp.broadcast_to(x[None], (peers, *x.shape)), axis, 0, 0, tiled=True)


def taken_together(x, axis):
    everything = copy_for_each(x, axis)
    return jnp.sum(everything, axis=0)


def packed_total(arrays, axis):
    ends = [0]
    for a in arrays:
        ends.append(ends[-1] + a.size)
    running = taken_together(jnp.concatenate([a.ravel() for a in arrays]), axis)
    return tuple((running[b:e].reshape(a.shape) for a, b, e in zip(arrays, ends, ends[1:])))


def body(patches, gain, shift, proj_weight, llm_rank, embed_grad):
    row_count = patches.shape[0]
    owned_width = patches.shape[1]
    width = gain.shape[0]
    out_cols = proj_weight.shape[1]
    column_start = lax.axis_index(("section", "llmdp")) * owned_width
    gain_own = lax.dynamic_slice_in_dim(gain, column_start, owned_width, 0)
    complete_rows = lax.all_gather(patches, ("section", "llmdp"), axis=1, tiled=True).astype(
        jnp.float32
    )
    row_average = jnp.mean(complete_rows, 1, keepdims=True)
    variance = jnp.mean(complete_rows * complete_rows, 1, keepdims=True) - row_average * row_average
    inverse_deviation = lax.rsqrt(variance + EPSILON)
    standardized_full = (complete_rows - row_average) * inverse_deviation
    normed_hidden = (standardized_full * gain + shift).astype(jnp.bfloat16)
    standardized_owned = lax.dynamic_slice_in_dim(standardized_full, column_start, owned_width, 1)
    weight_full = whole_of(proj_weight, ENC, 0)
    embed_acc = jnp.dot(normed_hidden, weight_full, preferred_element_type=jnp.float32)
    embed = embed_acc.astype(jnp.bfloat16)
    senders = lax.axis_size(ENC)
    most_slots = embed_grad.shape[0] // senders
    target = llm_rank[:, 0]
    owners = jnp.arange(senders, dtype=jnp.int32)
    hits = (target[:, None] == owners[None, :]).astype(jnp.int32)
    rank = jnp.sum((jnp.cumsum(hits, 0) - hits) * hits, 1)
    slot = target * most_slots + rank
    outgoing = jnp.zeros((senders * most_slots, out_cols), jnp.bfloat16).at[slot].set(embed)
    arrived = lax.all_to_all(
        outgoing.reshape(senders, most_slots, out_cols),
        ENC,
        split_axis=0,
        concat_axis=0,
        tiled=True,
    )
    embeds_recv = arrived.reshape(senders * most_slots, out_cols)
    returned = lax.all_to_all(
        embed_grad.reshape(senders, most_slots, out_cols),
        ENC,
        split_axis=0,
        concat_axis=0,
        tiled=True,
    )
    d_embed = returned.reshape(senders * most_slots, out_cols)[slot]
    partial_grad = lax.dot_general(
        d_embed, weight_full, (((1,), (1,)), ((), ())), preferred_element_type=jnp.float32
    )
    grad_weight = summed_rows(
        lax.dot_general(
            normed_hidden, d_embed, (((0,), (0,)), ((), ())), preferred_element_type=jnp.float32
        ),
        ENC,
    )
    group_count = width // owned_width
    pieces = partial_grad.astype(jnp.bfloat16).reshape(row_count, group_count, owned_width)
    columns = lax.all_to_all(pieces, ("section", "llmdp"), split_axis=1, concat_axis=1, tiled=True)
    owned_normalized_gradient = jnp.sum(columns.astype(jnp.float32), 1)
    owned_centered_gradient = owned_normalized_gradient * gain_own
    mean_sum, cross_sum = packed_total(
        (
            jnp.sum(owned_centered_gradient, 1),
            jnp.sum(owned_centered_gradient * standardized_owned, 1),
        ),
        ("section", "llmdp"),
    )
    gradient_row_average = (mean_sum / width)[:, None]
    gradient_cross_product = (cross_sum / width)[:, None]
    hidden_state_gradient = (
        inverse_deviation
        * (
            owned_centered_gradient
            - gradient_row_average
            - standardized_owned * gradient_cross_product
        )
    ).astype(jnp.bfloat16)
    gain_gradient, grad_shift = packed_total(
        (
            jnp.sum(owned_normalized_gradient * standardized_owned, 0),
            jnp.sum(owned_normalized_gradient, 0),
        ),
        ENC,
    )
    return (embeds_recv, hidden_state_gradient, grad_weight, gain_gradient, grad_shift)


def solution(mesh):
    split = Mesh(
        mesh.devices.reshape(8, 4, mesh.shape["section"], mesh.shape["llmdp"]),
        ("enc_0", "enc_1", "section", "llmdp"),
    )
    in_specs = (
        P(ENC, ("section", "llmdp")),
        P(),
        P(),
        P(ENC, ("section", "llmdp")),
        P(ENC, None),
        P(ENC, ("section", "llmdp")),
    )
    out_specs = (
        P(ENC, ("section", "llmdp")),
        P(ENC, ("section", "llmdp")),
        P(ENC, ("section", "llmdp")),
        P(("section", "llmdp")),
        P(("section", "llmdp")),
    )
    return jax.shard_map(body, mesh=split, in_specs=in_specs, out_specs=out_specs, check_vma=False)
```

profile of v0, /device:TPU:2, one launch (start us, length us, event | category | flops | bytes accessed | tf_op | source)
XLA Modules:
  0.0 333.3 jit_solution(10360011077139938337)
XLA Ops:
  7.2 0.7 all-gather.4.cloned.1.call-update
  8.0 15.6 %all-gather = bf16[4,100,512]{2,1,0:T(8,128)(2,1)S(1)} all-gather(bf16[1,100,512]{2,1,0:T(8,128)(2,1)} %bitcast.40), channel_id=1, replica_groups=mesh['enc_0'=8,'enc_1'=4,'section'=8,'llmdp'=2] {'enc_1'}, dimensions={0}, use_global_device_ids=true | all-gather | bytes 512000 | tf_op jit(solution)/shard_map/all_gather | solution.py:13
  23.5 0.8 reshape.100
  24.4 7.8 %all-to-all-start.1 = ((bf16[32,24,512]{2,1,0:T(8,128)(2,1)}), bf16[32,24,512]{2,1,0:T(8,128)(2,1)S(1)}, u32[]{:S(2)}, u32[]{:S(2)}) async-start(bf16[32,24,512]{2,1,0:T(8,128)(2,1)} %bitcast.39), calls=%async_computation.1 | async-start | bytes 1572864 | tf_op jit(solution)/shard_map/all_to_all | solution.py:77
  33.2 18.2 %all-to-all-done.1 = bf16[32,24,512]{2,1,0:T(8,128)(2,1)S(1)} async-done(((bf16[32,24,512]{2,1,0:T(8,128)(2,1)}), bf16[32,24,512]{2,1,0:T(8,128)(2,1)S(1)}, u32[]{:S(2)}, u32[]{:S(2)}) %all-to-all-start.1) | async-done | bytes 786464 | tf_op jit(solution)/shard_map/all_to_all | solution.py:77
  51.4 1.2 gather_fusion
  52.6 80.3 %all-gather.4.cloned.1.call-done = bf16[256,3200]{0,1:T(8,128)(2,1)} async-done(((bf16[256,200]{0,1:T(8,128)(2,1)}), bf16[256,3200]{0,1:T(8,128)(2,1)}) %all-gather.4.cloned.1.call-update) | async-done | bytes 1638416 | tf_op jit(solution)/shard_map/all_gather | solution.py:49
  132.9 1.9 convert_reduce_fusion
  134.8 4.2 %convolution_convert_fusion = bf16[3200,512]{1,0:T(8,128)(2,1)} fusion(bf16[256,512]{1,0:T(8,128)(2,1)S(1)} %gather_fusion, f32[3200]{0:T(1024)S(1)} %copy-done.3, f32[3200]{0:T(1024)S(1)} %copy-done.2, f32[256]{0:T(256)S(1)} %get-tuple-element.17, f32[256]{0:T(256)S(1)} %get-tuple-element.16, bf16[256,3200]{0,1:T(8,128)(2,1)} %all-gather.4.cloned.1.call-done), kind=kOutput, calls=%fused_computation.2 | convolution fusion | flops 845414400 | bytes 5204992 | tf_op jit(solution)/shard_map/dot_general | solution.py:89
  139.1 43.3 %all-gather.6.cloned.1.call-done = bf16[3200,512]{1,0:T(8,128)(2,1)} async-done(((bf16[400,512]{1,0:T(8,128)(2,1)}), bf16[3200,512]{1,0:T(8,128)(2,1)}) %all-gather.6.cloned.1.call-update) | async-done | bytes 3276816 | tf_op jit(solution)/shard_map/all_gather | solution.py:13
  182.3 4.1 %convolution_convert_fusion.2 = bf16[256,512]{1,0:T(8,128)(2,1)S(1)} fusion(bf16[3200,512]{1,0:T(8,128)(2,1)} %all-gather.6.cloned.1.call-done, f32[3200]{0:T(1024)S(1)} %copy-done.3, f32[3200]{0:T(1024)S(1)} %copy-done.2, f32[256]{0:T(256)S(1)} %get-tuple-element.17, f32[256]{0:T(256)S(1)} %get-tuple-element.16, bf16[256,3200]{0,1:T(8,128)(2,1)S(1)} %copy-done), kind=kOutput, calls=%fused_computation.12 | convolution fusion | flops 843907072 | bytes 5204992 | tf_op jit(solution)/shard_map/dot_general | solution.py:59
  186.4 2.5 scatter_custom_fusion
  188.9 7.6 %all-to-all-start = ((bf16[32,24,512]{2,1,0:T(8,128)(2,1)}), bf16[32,24,512]{2,1,0:T(8,128)(2,1)}, u32[]{:S(2)}, u32[]{:S(2)}) async-start(bf16[32,24,512]{2,1,0:T(8,128)(2,1)} %bitcast.6), calls=%async_computation | async-start | bytes 1572864 | tf_op jit(solution)/shard_map/all_to_all | solution.py:69
  196.5 3.0 convolution_convert_fusion.1
  199.5 2.2 copy.18
  201.8 25.3 %all-to-all-done = bf16[32,24,512]{2,1,0:T(8,128)(2,1)} async-done(((bf16[32,24,512]{2,1,0:T(8,128)(2,1)}), bf16[32,24,512]{2,1,0:T(8,128)(2,1)}, u32[]{:S(2)}, u32[]{:S(2)}) %all-to-all-start) | async-done | bytes 786464 | tf_op jit(solution)/shard_map/all_to_all | solution.py:69
  227.1 7.5 %all-to-all-start.2 = ((bf16[256,16,200]{0,2,1:T(8,128)(2,1)}), bf16[256,16,200]{0,2,1:T(8,128)(2,1)S(1)}, u32[]{:S(2)}, u32[]{:S(2)}) async-start(bf16[256,16,200]{0,2,1:T(8,128)(2,1)} %bitcast.38), calls=%async_computation.2 | async-start | bytes 3276800 | tf_op jit(solution)/shard_map/all_to_all | solution.py:96
  234.6 0.8 dynamic_slice.6
  235.4 1.3 dynamic-slice.4
  237.3 2.0 fusion.1
  239.4 36.7 %all-to-all-done.2 = bf16[256,16,200]{0,2,1:T(8,128)(2,1)S(1)} async-done(((bf16[256,16,200]{0,2,1:T(8,128)(2,1)}), bf16[256,16,200]{0,2,1:T(8,128)(2,1)S(1)}, u32[]{:S(2)}, u32[]{:S(2)}) %all-to-all-start.2) | async-done | bytes 1638432 | tf_op jit(solution)/shard_map/all_to_all | solution.py:96
  276.5 1.1 multiply_reduce_fusion
  278.2 3.5 %all-to-all-start.3 = ((f32[16,1,512]{2,1,0:T(1,128)}), f32[16,1,512]{2,1,0:T(1,128)S(1)}, u32[]{:S(2)}, u32[]{:S(2)}) async-start(f32[16,1,512]{2,1,0:T(1,128)} %broadcast_in_dim.7), calls=%async_computation.3 | async-start | bytes 65536 | tf_op jit(solution)/shard_map/all_to_all | solution.py:26
  281.8 7.6 %all-to-all-done.3 = f32[16,1,512]{2,1,0:T(1,128)S(1)} async-done(((f32[16,1,512]{2,1,0:T(1,128)}), f32[16,1,512]{2,1,0:T(1,128)S(1)}, u32[]{:S(2)}, u32[]{:S(2)}) %all-to-all-start.3) | async-done | bytes 32800 | tf_op jit(solution)/shard_map/all_to_all | solution.py:26
  290.1 5.3 %all-to-all-start.4 = ((f32[32,1,400]{2,1,0:T(1,128)}), f32[32,1,400]{2,1,0:T(1,128)S(1)}, u32[]{:S(2)}, u32[]{:S(2)}) async-start(f32[32,1,400]{2,1,0:T(1,128)} %broadcast_in_dim.8), calls=%async_computation.5 | async-start | bytes 131072 | tf_op jit(solution)/shard_map/all_to_all | solution.py:26
  295.4 1.7 multiply_convert_fusion
  297.1 7.0 %all-to-all-done.4 = f32[32,1,400]{2,1,0:T(1,128)S(1)} async-done(((f32[32,1,400]{2,1,0:T(1,128)}), f32[32,1,400]{2,1,0:T(1,128)S(1)}, u32[]{:S(2)}, u32[]{:S(2)}) %all-to-all-start.4) | async-done | bytes 51232 | tf_op jit(solution)/shard_map/all_to_all | solution.py:26
  304.1 14.1 %fusion = bf16[104,512]{1,0:T(8,128)(2,1)S(1)} fusion(bf16[400,512]{1,0:T(8,128)(2,1)} %reduce-scatter.4.cloned.1.call-done), kind=kCustom, calls=%all-reduce-scatter | all-reduce-scatter fusion | flops 212993 | bytes 518144
  318.2 2.6 collective-permute-start
  321.4 2.4 collective-permute-done
  324.0 0.7 dynamic-slice_convert_fusion
  324.7 2.1 copy.30
  (34 shorter events, 3.8 us)
Async XLA Ops:
  7.2 25.1 %copy-start.1 = (s32[256,1]{0,1:T(1,128)S(1)}, s32[256,1]{0,1:T(1,128)}, u32[]{:S(2)}) copy-start(s32[256,1]{0,1:T(1,128)} %param.10) | copy-start | bytes 3076
  7.2 125.7 %all-gather.4.cloned.1.call-start = ((), (), s32[]{:S(2)}) async-start(), calls=%async_computation.6 | async-start | bytes 1740800 | tf_op jit(solution)/shard_map/all_gather | solution.py:49
  7.9 174.4 %all-gather.6.cloned.1.call-start = ((), (), s32[]{:S(2)}) async-start(), calls=%async_computation.7 | async-start | bytes 3686400 | tf_op jit(solution)/shard_map/all_gather | solution.py:13
  24.3 110.5 %copy-start.2 = (f32[3200]{0:T(1024)S(1)}, f32[3200]{0:T(1024)}, u32[]{:S(2)}) copy-start(f32[3200]{0:T(1024)} %param.7) | copy-start | bytes 38404
  24.3 110.5 %copy-start.3 = (f32[3200]{0:T(1024)S(1)}, f32[3200]{0:T(1024)}, u32[]{:S(2)}) copy-start(f32[3200]{0:T(1024)} %param.8) | copy-start | bytes 38404
  24.4 27.1 %all-to-all-start.1 = ((bf16[32,24,512]{2,1,0:T(8,128)(2,1)}), bf16[32,24,512]{2,1,0:T(8,128)(2,1)S(1)}, u32[]{:S(2)}, u32[]{:S(2)}) async-start(bf16[32,24,512]{2,1,0:T(8,128)(2,1)} %bitcast.39), calls=%async_computation.1 | async-start | bytes 1572864 | tf_op jit(solution)/shard_map/all_to_all | solution.py:77
  32.2 271.9 %reduce-scatter.4.cloned.1.call-start = ((), (), s32[]{:S(2)}) async-start(), calls=%async_computation.8 | async-start | bytes 3686400 | tf_op jit(solution)/shard_map/reduce_scatter | solution.py:20
  139.0 43.3 %copy-start = (bf16[256,3200]{0,1:T(8,128)(2,1)S(1)}, bf16[256,3200]{0,1:T(8,128)(2,1)}, u32[]{:S(2)}) copy-start(bf16[256,3200]{0,1:T(8,128)(2,1)} %all-gather.4.cloned.1.call-done) | copy-start | bytes 4915204
  188.9 38.3 %all-to-all-start = ((bf16[32,24,512]{2,1,0:T(8,128)(2,1)}), bf16[32,24,512]{2,1,0:T(8,128)(2,1)}, u32[]{:S(2)}, u32[]{:S(2)}) async-start(bf16[32,24,512]{2,1,0:T(8,128)(2,1)} %bitcast.6), calls=%async_computation | async-start | bytes 1572864 | tf_op jit(solution)/shard_map/all_to_all | solution.py:69
  227.1 49.0 %all-to-all-start.2 = ((bf16[256,16,200]{0,2,1:T(8,128)(2,1)}), bf16[256,16,200]{0,2,1:T(8,128)(2,1)S(1)}, u32[]{:S(2)}, u32[]{:S(2)}) async-start(bf16[256,16,200]{0,2,1:T(8,128)(2,1)} %bitcast.38), calls=%async_computation.2 | async-start | bytes 3276800 | tf_op jit(solution)/shard_map/all_to_all | solution.py:96
  278.2 11.2 %all-to-all-start.3 = ((f32[16,1,512]{2,1,0:T(1,128)}), f32[16,1,512]{2,1,0:T(1,128)S(1)}, u32[]{:S(2)}, u32[]{:S(2)}) async-start(f32[16,1,512]{2,1,0:T(1,128)} %broadcast_in_dim.7), calls=%async_computation.3 | async-start | bytes 65536 | tf_op jit(solution)/shard_map/all_to_all | solution.py:26
  290.1 14.0 %all-to-all-start.4 = ((f32[32,1,400]{2,1,0:T(1,128)}), f32[32,1,400]{2,1,0:T(1,128)S(1)}, u32[]{:S(2)}, u32[]{:S(2)}) async-start(f32[32,1,400]{2,1,0:T(1,128)} %broadcast_in_dim.8), calls=%async_computation.5 | async-start | bytes 131072 | tf_op jit(solution)/shard_map/all_to_all | solution.py:26
  318.2 5.6 %collective-permute-start = (bf16[12,512]{1,0:T(8,128)(2,1)S(1)}, bf16[12,512]{1,0:T(8,128)(2,1)S(1)}, u32[]{:S(2)}, u32[]{:S(2)}) collective-permute-start(bf16[12,512]{1,0:T(8,128)(2,1)S(1)} %slice.27), channel_id=1, source_target_pairs={{0,16},{16,32},{32,48},{1,17},{17,33},{33,49},{2,18},{18,34},{34,5... | collective-permute-start | bytes 36872
Sparse Core Ops, SparseCore 0:
  10.1 122.7 all-gather.3
  135.6 46.7 all-gather.5
  185.2 62.8 reduce-scatter.3
where the time goes:
time: 334 us; the launch traced here: 333 us
  waiting for transfers between devices  222 us (66%)
  starting transfers between devices  34.4 us (10%)
  blocking collectives  29.6 us (9%)
  between operations  14.6 us (4%)
  local copies, waits for them, and re-layouts  13.1 us (4%)
  matrix products  11.3 us (3%)
  other arithmetic  8.74 us (3%)
    all_gather x1, waiting for transfers between devices, body(): lax.all_gather(patches, ('section', 'llmdp'), axis=1, tiled=True)  80.3 us
    all_gather x1, waiting for transfers between devices, whole_of(): x = lax.all_gather(x, axis, axis=dim, tiled=True)  43.3 us
    all_to_all x1, waiting for transfers between devices, body(): lax.all_to_all(pieces, ('section', 'llmdp'), split_axis=1, concat_axis=1,...  36.7 us
    all_to_all x1, waiting for transfers between devices, body(): lax.all_to_all(outgoing.reshape(senders, most_slots, out_cols), ENC, spli...  25.3 us
    all_to_all x1, waiting for transfers between devices, body(): lax.all_to_all(embed_grad.reshape(senders, most_slots, out_cols), ENC, sp...  18.2 us
    all_gather x1, blocking collectives, whole_of(): x = lax.all_gather(x, axis, axis=dim, tiled=True)  15.6 us
    all_to_all x2, waiting for transfers between devices, copy_for_each(): lax.all_to_all(jnp.broadcast_to(x[None], (peers, *x.shape)), axis, 0, 0,...  14.6 us
    unnamed x1, blocking collectives  14.1 us
  transfers between devices with their start and end apart: 9, of which 8 were waited for; matrix products, arithmetic and copies ran while one was open for 9% of the time, Pallas kernels for 0%

commit v1 on v0

--- a/solution.py
+++ b/solution.py
@@ -93,7 +93,15 @@
     )
     group_count = width // owned_width
     pieces = partial_grad.astype(jnp.bfloat16).reshape(row_count, group_count, owned_width)
-    columns = lax.all_to_all(pieces, ("section", "llmdp"), split_axis=1, concat_axis=1, tiled=True)
+    columns = jnp.concatenate(
+        lax.all_to_all(
+            jnp.stack(jnp.split(pieces, lax.axis_size(("section", "llmdp")), axis=1)),
+            ("section", "llmdp"),
+            0,
+            0,
+        ),
+        axis=1,
+    )
     owned_normalized_gradient = jnp.sum(columns.astype(jnp.float32), 1)
     owned_centered_gradient = owned_normalized_gradient * gain_own
     mean_sum, cross_sum = packed_total(

time: 334 us -> 333 us (level)
  waiting for transfers between devices: 222 us -> 212 us
  local copies, waits for them, and re-layouts: 13.1 us -> 21.7 us
    all_to_all x1, waiting for transfers between devices: 25.3 us -> 16.6 us  [body(): lax.all_to_all(outgoing.reshape(senders, most_slots, out_cols), ENC, spli...]
    unnamed x13 -> x32, local copies, waits for them, and re-layouts: 4.35 us -> 12.9 us
    all_gather x1, waiting for transfers between devices: 80.3 us -> 73.3 us  [body(): lax.all_gather(patches, ('section', 'llmdp'), axis=1, tiled=True)]
    all_gather x1, waiting for transfers between devices: 43.3 us -> 49.5 us  [whole_of(): x = lax.all_gather(x, axis, axis=dim, tiled=True)]
  transfers between devices with their start and end apart: 9 -> 9, of which waited for: 8 -> 8; matrix products, arithmetic and copies ran while one was open for 9% -> 11% of each run, Pallas kernels for 0% -> 0%
where the time goes in v1:
time: 333 us; the launch traced here: 332 us
  waiting for transfers between devices  212 us (64%)
  starting transfers between devices  34.4 us (10%)
  blocking collectives  29.6 us (9%)
  local copies, waits for them, and re-layouts  21.7 us (7%)
  between operations  14.7 us (4%)
  matrix products  10.3 us (3%)
  other arithmetic  8.86 us (3%)
    all_gather x1, waiting for transfers between devices, body(): lax.all_gather(patches, ('section', 'llmdp'), axis=1, tiled=True)  73.3 us
    all_gather x1, waiting for transfers between devices, whole_of(): x = lax.all_gather(x, axis, axis=dim, tiled=True)  49.5 us
    all_to_all x1, waiting for transfers between devices, body(): lax.all_to_all(jnp.stack(jnp.split(pieces, lax.axis_size(('section', 'llm...  36.7 us
    all_to_all x1, waiting for transfers between devices, body(): lax.all_to_all(embed_grad.reshape(senders, most_slots, out_cols), ENC, sp...  18.2 us
    all_to_all x1, waiting for transfers between devices, body(): lax.all_to_all(outgoing.reshape(senders, most_slots, out_cols), ENC, spli...  16.6 us
    all_gather x1, blocking collectives, whole_of(): x = lax.all_gather(x, axis, axis=dim, tiled=True)  15.6 us
    all_to_all x2, waiting for transfers between devices, copy_for_each(): lax.all_to_all(jnp.broadcast_to(x[None], (peers, *x.shape)), axis, 0, 0,...  14.6 us
    unnamed x1, blocking collectives  14.1 us
  transfers between devices with their start and end apart: 9, of which 8 were waited for; matrix products, arithmetic and copies ran while one was open for 11% of the time, Pallas kernels for 0%

profile of v1, /device:TPU:2, one launch (start us, length us, event | category | flops | bytes accessed | tf_op | source)
XLA Modules:
  0.0 331.6 jit_solution(7865586624540790409)
XLA Ops:
  8.0 15.6 %all-gather = bf16[4,100,512]{2,1,0:T(8,128)(2,1)S(1)} all-gather(bf16[1,100,512]{2,1,0:T(8,128)(2,1)} %bitcast.117), channel_id=1, replica_groups=mesh['enc_0'=8,'enc_1'=4,'section'=8,'llmdp'=2] {'enc_1'}, dimensions={0}, use_global_device_ids=true | all-gather | bytes 512000 | tf_op jit(solution)/shard_map/all_gather | solution.py:13
  24.4 7.8 %all-to-all-start.1 = ((bf16[32,24,512]{2,1,0:T(8,128)(2,1)}), bf16[32,24,512]{2,1,0:T(8,128)(2,1)S(1)}, u32[]{:S(2)}, u32[]{:S(2)}) async-start(bf16[32,24,512]{2,1,0:T(8,128)(2,1)} %bitcast.8), calls=%async_computation.1 | async-start | bytes 1572864 | tf_op jit(solution)/shard_map/all_to_all | solution.py:77
  33.2 18.2 %all-to-all-done.1 = bf16[32,24,512]{2,1,0:T(8,128)(2,1)S(1)} async-done(((bf16[32,24,512]{2,1,0:T(8,128)(2,1)}), bf16[32,24,512]{2,1,0:T(8,128)(2,1)S(1)}, u32[]{:S(2)}, u32[]{:S(2)}) %all-to-all-start.1) | async-done | bytes 786464 | tf_op jit(solution)/shard_map/all_to_all | solution.py:77
  51.4 1.2 gather_fusion
  52.6 73.3 %all-gather.4.cloned.1.call-done = bf16[256,3200]{0,1:T(8,128)(2,1)} async-done(((bf16[256,200]{0,1:T(8,128)(2,1)}), bf16[256,3200]{0,1:T(8,128)(2,1)}) %all-gather.4.cloned.1.call-update) | async-done | bytes 1638416 | tf_op jit(solution)/shard_map/all_gather | solution.py:49
  125.9 2.0 convert_reduce_fusion
  128.0 3.2 convolution_convert_fusion
  131.2 49.5 %all-gather.6.cloned.1.call-done = bf16[3200,512]{1,0:T(8,128)(2,1)} async-done(((bf16[400,512]{1,0:T(8,128)(2,1)}), bf16[3200,512]{1,0:T(8,128)(2,1)}) %all-gather.6.cloned.1.call-update) | async-done | bytes 3276816 | tf_op jit(solution)/shard_map/all_gather | solution.py:13
  180.7 4.1 %convolution_convert_fusion.2 = bf16[256,512]{1,0:T(8,128)(2,1)S(1)} fusion(bf16[3200,512]{1,0:T(8,128)(2,1)} %all-gather.6.cloned.1.call-done, f32[3200]{0:T(1024)S(1)} %copy-done.5, f32[3200]{0:T(1024)S(1)} %copy-done.4, f32[256]{0:T(256)S(1)} %get-tuple-element.17, f32[256]{0:T(256)S(1)} %get-tuple-element.16, bf16[256,3200]{0,1:T(8,128)(2,1)S(1)} %copy-done), kind=kOutput, calls=%fused_computation.12 | convolution fusion | flops 843907072 | bytes 5204992 | tf_op jit(solution)/shard_map/dot_general | solution.py:59
  184.7 2.5 scatter_custom_fusion
  187.2 7.6 %all-to-all-start = ((bf16[32,24,512]{2,1,0:T(8,128)(2,1)}), bf16[32,24,512]{2,1,0:T(8,128)(2,1)}, u32[]{:S(2)}, u32[]{:S(2)}) async-start(bf16[32,24,512]{2,1,0:T(8,128)(2,1)} %bitcast.6), calls=%async_computation | async-start | bytes 1572864 | tf_op jit(solution)/shard_map/all_to_all | solution.py:69
  194.9 3.1 convolution_convert_fusion.1
  197.9 2.3 copy.33
  200.2 1.0 fusion.20
  203.9 0.9 fusion.16
  204.8 0.9 fusion.15
  207.7 1.2 copy-done.2
  208.9 16.6 %all-to-all-done = bf16[32,24,512]{2,1,0:T(8,128)(2,1)} async-done(((bf16[32,24,512]{2,1,0:T(8,128)(2,1)}), bf16[32,24,512]{2,1,0:T(8,128)(2,1)}, u32[]{:S(2)}, u32[]{:S(2)}) %all-to-all-start) | async-done | bytes 786464 | tf_op jit(solution)/shard_map/all_to_all | solution.py:69
  225.5 7.5 %all-to-all-start.2 = ((bf16[16,256,1,200]{1,3,2,0:T(8,128)(2,1)}), bf16[16,256,1,200]{1,3,2,0:T(8,128)(2,1)S(1)}, u32[]{:S(2)}, u32[]{:S(2)}) async-start(bf16[16,256,1,200]{1,3,2,0:T(8,128)(2,1)} %copy-done.2), calls=%async_computation.2 | async-start | bytes 3276800 | tf_op jit(solution)/shard_map/all_to_all | solution.py:97
  233.8 1.3 dynamic-slice.4
  235.7 2.0 fusion.1
  237.7 36.7 %all-to-all-done.2 = bf16[16,256,1,200]{1,3,2,0:T(8,128)(2,1)S(1)} async-done(((bf16[16,256,1,200]{1,3,2,0:T(8,128)(2,1)}), bf16[16,256,1,200]{1,3,2,0:T(8,128)(2,1)S(1)}, u32[]{:S(2)}, u32[]{:S(2)}) %all-to-all-start.2) | async-done | bytes 1638432 | tf_op jit(solution)/shard_map/all_to_all | solution.py:97
  274.8 1.1 multiply_reduce_fusion
  276.5 3.5 %all-to-all-start.3 = ((f32[16,1,512]{2,1,0:T(1,128)}), f32[16,1,512]{2,1,0:T(1,128)S(1)}, u32[]{:S(2)}, u32[]{:S(2)}) async-start(f32[16,1,512]{2,1,0:T(1,128)} %broadcast_in_dim.7), calls=%async_computation.3 | async-start | bytes 65536 | tf_op jit(solution)/shard_map/all_to_all | solution.py:26
  280.1 7.6 %all-to-all-done.3 = f32[16,1,512]{2,1,0:T(1,128)S(1)} async-done(((f32[16,1,512]{2,1,0:T(1,128)}), f32[16,1,512]{2,1,0:T(1,128)S(1)}, u32[]{:S(2)}, u32[]{:S(2)}) %all-to-all-start.3) | async-done | bytes 32800 | tf_op jit(solution)/shard_map/all_to_all | solution.py:26
  288.4 5.2 %all-to-all-start.4 = ((f32[32,1,400]{2,1,0:T(1,128)}), f32[32,1,400]{2,1,0:T(1,128)S(1)}, u32[]{:S(2)}, u32[]{:S(2)}) async-start(f32[32,1,400]{2,1,0:T(1,128)} %broadcast_in_dim.8), calls=%async_computation.5 | async-start | bytes 131072 | tf_op jit(solution)/shard_map/all_to_all | solution.py:26
  293.7 1.7 multiply_convert_fusion
  295.4 7.0 %all-to-all-done.4 = f32[32,1,400]{2,1,0:T(1,128)S(1)} async-done(((f32[32,1,400]{2,1,0:T(1,128)}), f32[32,1,400]{2,1,0:T(1,128)S(1)}, u32[]{:S(2)}, u32[]{:S(2)}) %all-to-all-start.4) | async-done | bytes 51232 | tf_op jit(solution)/shard_map/all_to_all | solution.py:26
  302.4 14.1 %fusion = bf16[104,512]{1,0:T(8,128)(2,1)S(1)} fusion(bf16[400,512]{1,0:T(8,128)(2,1)} %reduce-scatter.4.cloned.1.call-done), kind=kCustom, calls=%all-reduce-scatter | all-reduce-scatter fusion | flops 212993 | bytes 518144
  316.5 2.6 collective-permute-start
  319.8 2.4 collective-permute-done
  323.0 2.1 copy.60
  (54 shorter events, 11.4 us)
Async XLA Ops:
  7.2 118.8 %all-gather.4.cloned.1.call-start = ((), (), s32[]{:S(2)}) async-start(), calls=%async_computation.6 | async-start | bytes 1740800 | tf_op jit(solution)/shard_map/all_gather | solution.py:49
  7.9 172.8 %all-gather.6.cloned.1.call-start = ((), (), s32[]{:S(2)}) async-start(), calls=%async_computation.7 | async-start | bytes 3686400 | tf_op jit(solution)/shard_map/all_gather | solution.py:13
  7.9 24.3 %copy-start.3 = (s32[256,1]{0,1:T(1,128)S(1)}, s32[256,1]{0,1:T(1,128)}, u32[]{:S(2)}) copy-start(s32[256,1]{0,1:T(1,128)} %param.10) | copy-start | bytes 3076
  24.4 27.1 %all-to-all-start.1 = ((bf16[32,24,512]{2,1,0:T(8,128)(2,1)}), bf16[32,24,512]{2,1,0:T(8,128)(2,1)S(1)}, u32[]{:S(2)}, u32[]{:S(2)}) async-start(bf16[32,24,512]{2,1,0:T(8,128)(2,1)} %bitcast.8), calls=%async_computation.1 | async-start | bytes 1572864 | tf_op jit(solution)/shard_map/all_to_all | solution.py:77
  32.2 270.3 %reduce-scatter.4.cloned.1.call-start = ((), (), s32[]{:S(2)}) async-start(), calls=%async_computation.8 | async-start | bytes 3686400 | tf_op jit(solution)/shard_map/reduce_scatter | solution.py:20
  51.4 76.5 %copy-start.4 = (f32[3200]{0:T(1024)S(1)}, f32[3200]{0:T(1024)}, u32[]{:S(2)}) copy-start(f32[3200]{0:T(1024)} %param.7) | copy-start | bytes 38404
  51.4 76.5 %copy-start.5 = (f32[3200]{0:T(1024)S(1)}, f32[3200]{0:T(1024)}, u32[]{:S(2)}) copy-start(f32[3200]{0:T(1024)} %param.8) | copy-start | bytes 38404
  125.9 2.1 copy-start
  187.2 38.3 %all-to-all-start = ((bf16[32,24,512]{2,1,0:T(8,128)(2,1)}), bf16[32,24,512]{2,1,0:T(8,128)(2,1)}, u32[]{:S(2)}, u32[]{:S(2)}) async-start(bf16[32,24,512]{2,1,0:T(8,128)(2,1)} %bitcast.6), calls=%async_computation | async-start | bytes 1572864 | tf_op jit(solution)/shard_map/all_to_all | solution.py:69
  200.2 7.3 %copy-start.1 = (bf16[256,3200]{0,1:T(8,128)(2,1)S(1)}, bf16[256,3200]{0,1:T(8,128)(2,1)}, u32[]{:S(2)}) copy-start(bf16[256,3200]{0,1:T(8,128)(2,1)} %copy.33) | copy-start | bytes 4915204
  207.7 1.2 copy-start.2
  225.5 49.0 %all-to-all-start.2 = ((bf16[16,256,1,200]{1,3,2,0:T(8,128)(2,1)}), bf16[16,256,1,200]{1,3,2,0:T(8,128)(2,1)S(1)}, u32[]{:S(2)}, u32[]{:S(2)}) async-start(bf16[16,256,1,200]{1,3,2,0:T(8,128)(2,1)} %copy-done.2), calls=%async_computation.2 | async-start | bytes 3276800 | tf_op jit(solution)/shard_map/all_to_all | solution.py:97
  276.5 11.2 %all-to-all-start.3 = ((f32[16,1,512]{2,1,0:T(1,128)}), f32[16,1,512]{2,1,0:T(1,128)S(1)}, u32[]{:S(2)}, u32[]{:S(2)}) async-start(f32[16,1,512]{2,1,0:T(1,128)} %broadcast_in_dim.7), calls=%async_computation.3 | async-start | bytes 65536 | tf_op jit(solution)/shard_map/all_to_all | solution.py:26
  288.4 13.9 %all-to-all-start.4 = ((f32[32,1,400]{2,1,0:T(1,128)}), f32[32,1,400]{2,1,0:T(1,128)S(1)}, u32[]{:S(2)}, u32[]{:S(2)}) async-start(f32[32,1,400]{2,1,0:T(1,128)} %broadcast_in_dim.8), calls=%async_computation.5 | async-start | bytes 131072 | tf_op jit(solution)/shard_map/all_to_all | solution.py:26
  316.5 5.6 %collective-permute-start = (bf16[12,512]{1,0:T(8,128)(2,1)S(1)}, bf16[12,512]{1,0:T(8,128)(2,1)S(1)}, u32[]{:S(2)}, u32[]{:S(2)}) collective-permute-start(bf16[12,512]{1,0:T(8,128)(2,1)S(1)} %slice.27), channel_id=1, source_target_pairs={{0,16},{16,32},{32,48},{1,17},{17,33},{33,49},{2,18},{18,34},{34,5... | collective-permute-start | bytes 36872
Sparse Core Ops, SparseCore 0:
  10.1 115.7 all-gather.3
  128.6 52.0 all-gather.5
  183.5 62.8 reduce-scatter.3
